TPU v7x, 256 devices: a whole 4x4x8 slice. The times are simulated.
256 devices in a mesh: dp: 32 (over x, z_hi, core), tensor: 8 (over y, z_lo).
Axes of the slice: x: 4, y: 4, z: 8 (z_hi: 4, z_lo: 2; z = z_hi * 2 + z_lo), core: 2. Of those that a mesh axis runs over, the one named last changes fastest.
Arguments:
- tokens: bfloat16 [64, 192, 4096], P('dp', None, 'tensor'), may hold values from -6 to 6
- grad_out: bfloat16 [64, 192, 4096], P('dp', None, 'tensor'), may hold values from -6 to 6
- counts: int32 [32], replicated, may hold values from 0 to 2, as said below
- gain: bfloat16 [4096], P('dp'), may hold values from 0.5 to 1.5
- wq: bfloat16 [4096, 4096], P('dp', 'tensor'), may hold values from -2.5 to 2.5
- wk: bfloat16 [4096, 1024], P('dp', 'tensor'), may hold values from -0.09375 to 0.09375
- wv: bfloat16 [4096, 1024], P('dp', 'tensor'), may hold values from -0.09375 to 0.09375
- wo: bfloat16 [4096, 4096], P('tensor', 'dp'), may hold values from -0.09375 to 0.09375
Outputs:
- mixed: bfloat16 [64, 192, 4096], P('dp', None, 'tensor')
- grad_tokens: bfloat16 [64, 192, 4096], P('dp', None, 'tensor')
- grad_gain: float32 [4096], P('dp')
- grad_wq: float32 [4096, 4096], P('dp', 'tensor')
- grad_wk: float32 [4096, 1024], P('dp', 'tensor')
- grad_wv: float32 [4096, 1024], P('dp', 'tensor')
- grad_wo: float32 [4096, 4096], P('tensor', 'dp')
Inputs may be any that keep to these rules, and one draw needn't show every extreme that they name: `counts`: replica r and replica r + 16 hold 2 live blocks together; in every draw some replica holds 2.
All inputs are finite; a program needn't handle non-finite values.
Results may differ from a plain program's by a relative error of at most 0.025.
Values may be sent and summed in bfloat16 or wider, within the bound.
No kernel may reach another device: no remote copies, remote signals or barrier semaphores. Data moves between devices by JAX's collectives and lax.ppermute only.
A program may use at most 128 MiB of HBM per device.

v0:
```python
import jax
import jax.numpy as jnp
from jax import lax
from jax.sharding import PartitionSpec as P

HEADS = 32
KV = 8
HD = 128
epsilon = 1e-05


def attention_forward(query_heads, key_heads, value_heads):
    length = query_heads.shape[1]
    score_scale = query_heads.shape[-1] ** (-0.5)
    position = jnp.arange(length)
    causal = position[None, :] <= position[:, None]
    scores = (
        jnp.einsum("btgrh,bugh->bgrtu", query_heads, key_heads, preferred_element_type=jnp.float32)
        * score_scale
    )
    scores = jnp.where(causal, scores, -1e30)
    row_max = jnp.max(scores, axis=-1, keepdims=True)
    exp_scores = jnp.exp(scores - row_max)
    softmax_out = exp_scores / jnp.sum(exp_scores, axis=-1, keepdims=True)
    softmax_low = softmax_out.astype(jnp.bfloat16)
    context = jnp.einsum(
        "bgrtu,bugh->btgrh", softmax_low, value_heads, preferred_element_type=jnp.float32
    ).astype(jnp.bfloat16)
    return (softmax_out, softmax_low, context)


def attention_backward(grad_context, query_heads, key_heads, value_heads, softmax_out, softmax_low):
    score_scale = query_heads.shape[-1] ** (-0.5)
    grad_soft = jnp.einsum(
        "btgrh,bugh->bgrtu", grad_context, value_heads, preferred_element_type=jnp.float32
    )
    row_inner = jnp.sum(grad_soft * softmax_out, axis=-1, keepdims=True)
    grad_scores = (softmax_out * (grad_soft - row_inner) * score_scale).astype(jnp.bfloat16)
    grad_query = jnp.einsum(
        "bgrtu,bugh->btgrh", grad_scores, key_heads, preferred_element_type=jnp.float32
    ).astype(jnp.bfloat16)
    grad_key = jnp.einsum(
        "bgrtu,btgrh->bugh", grad_scores, query_heads, preferred_element_type=jnp.float32
    ).astype(jnp.bfloat16)
    grad_value = jnp.einsum(
        "bgrtu,btgrh->bugh", softmax_low, grad_context, preferred_element_type=jnp.float32
    ).astype(jnp.bfloat16)
    return (grad_query, grad_key, grad_value)


def on_device(tokens, grad_out, counts, gain, wq, wk, wv, wo):
    groups = lax.axis_size("tensor")
    dp_size = lax.axis_size("dp")
    replica = lax.axis_index("dp")
    own_count = counts[replica]
    blocks, length, shard_width = tokens.shape
    full_width = shard_width * groups
    d_local = gain.shape[0]
    q_cols = wq.shape[1]
    k_cols = wk.shape[1]
    o_rows = wo.shape[0]
    lane = wo.shape[1]
    pack = jnp.concatenate(
        [
            jnp.pad(gain.reshape(1, d_local), ((0, 7), (0, 0))),
            wq.reshape(d_local * q_cols // lane, lane),
            wk.reshape(d_local * k_cols // lane, lane),
            wv.reshape(d_local * k_cols // lane, lane),
            wo,
        ],
        axis=0,
    )
    packed = lax.all_gather(pack, "dp", axis=0, tiled=False)
    r0 = 8
    r1 = r0 + d_local * q_cols // lane
    r2 = r1 + d_local * k_cols // lane
    r3 = r2 + d_local * k_cols // lane
    r4 = r3 + o_rows
    gain_all = packed[:, 0, :].reshape(full_width)
    wq_all = packed[:, r0:r1, :].reshape(dp_size * d_local, q_cols)
    wk_all = packed[:, r1:r2, :].reshape(dp_size * d_local, k_cols)
    wv_all = packed[:, r2:r3, :].reshape(dp_size * d_local, k_cols)
    wo_blk = packed[:, r3:r4, :]
    live_mask = (jnp.arange(blocks) < own_count).astype(jnp.bfloat16)[:, None, None]
    block_grad = grad_out * live_mask
    both = lax.all_gather(jnp.stack([tokens, block_grad]), "tensor", axis=3, tiled=True)
    wide_in, upstream = (both[0], both[1])
    repeat = HEADS // KV
    kv_local = wk_all.shape[1] // HD
    wide_float = wide_in.astype(jnp.float32)
    inverse_rms = lax.rsqrt(jnp.mean(wide_float * wide_float, axis=-1, keepdims=True) + epsilon)
    unit_rows = wide_float * inverse_rms
    gain_float = gain_all.astype(jnp.float32)
    normed_float = unit_rows * gain_float
    normed = normed_float.astype(jnp.bfloat16)
    queries = jnp.einsum("btd,dk->btk", normed, wq_all, preferred_element_type=jnp.float32).astype(
        jnp.bfloat16
    )
    key_rows = jnp.einsum("btd,dk->btk", normed, wk_all, preferred_element_type=jnp.float32).astype(
        jnp.bfloat16
    )
    values = jnp.einsum("btd,dk->btk", normed, wv_all, preferred_element_type=jnp.float32).astype(
        jnp.bfloat16
    )
    query_heads = queries.reshape(blocks, length, kv_local, repeat, HD)
    key_heads = key_rows.reshape(blocks, length, kv_local, HD)
    value_heads = values.reshape(blocks, length, kv_local, HD)
    softmax_out, softmax_low, context = attention_forward(query_heads, key_heads, value_heads)
    context_flat = context.reshape(blocks, length, kv_local * repeat * HD)
    partial_value = jnp.einsum(
        "btk,jkl->btjl", context_flat, wo_blk, preferred_element_type=jnp.float32
    ).reshape(blocks, length, full_width)
    upstream_blk = upstream.reshape(blocks, length, dp_size, lane)
    grad_context = jnp.einsum(
        "btjl,jkl->btk", upstream_blk, wo_blk, preferred_element_type=jnp.float32
    ).astype(jnp.bfloat16)
    grad_output_proj = jnp.einsum(
        "btk,btjl->jkl", context_flat, upstream_blk, preferred_element_type=jnp.float32
    )
    grad_query, grad_key, grad_value = attention_backward(
        grad_context.reshape(blocks, length, kv_local, repeat, HD),
        query_heads,
        key_heads,
        value_heads,
        softmax_out,
        softmax_low,
    )
    grad_query = grad_query.reshape(blocks, length, -1)
    grad_key = grad_key.reshape(blocks, length, -1)
    grad_value = grad_value.reshape(blocks, length, -1)
    normed_terms = jnp.einsum("btk,dk->btd", grad_query, wq_all, preferred_element_type=jnp.float32)
    normed_terms = normed_terms + jnp.einsum(
        "btk,dk->btd", grad_key, wk_all, preferred_element_type=jnp.float32
    )
    normed_terms = normed_terms + jnp.einsum(
        "btk,dk->btd", grad_value, wv_all, preferred_element_type=jnp.float32
    )
    grad_query_proj = jnp.einsum(
        "btd,btk->dk", normed, grad_query, preferred_element_type=jnp.float32
    )
    grad_key_proj = jnp.einsum("btd,btk->dk", normed, grad_key, preferred_element_type=jnp.float32)
    grad_value_proj = jnp.einsum(
        "btd,btk->dk", normed, grad_value, preferred_element_type=jnp.float32
    )
    term_low = normed_terms.astype(jnp.bfloat16)
    term_float = term_low.astype(jnp.float32)
    rows = blocks * length
    row_dot = jnp.sum(term_float * normed_float, axis=-1).reshape(rows)
    gain_part = jnp.sum(term_float * unit_rows, axis=(0, 1))
    extra_rows = 1 + full_width // shard_width
    extra = jnp.concatenate(
        [
            jnp.pad(row_dot, (0, shard_width - rows)).reshape(1, shard_width),
            gain_part.reshape(full_width // shard_width, shard_width),
        ],
        axis=0,
    )
    extra_pad = -extra_rows % 8
    extra = jnp.pad(extra, ((0, extra_pad), (0, 0))).astype(jnp.bfloat16)

    def by_chunk(x):
        return x.reshape(rows, groups, shard_width).transpose(1, 0, 2)

    payload = jnp.concatenate(
        [
            by_chunk(partial_value.astype(jnp.bfloat16)),
            by_chunk(term_low),
            jnp.broadcast_to(extra[None], (groups,) + extra.shape),
        ],
        axis=1,
    )
    reduced = lax.psum_scatter(payload, "tensor", scatter_dimension=0, tiled=True)[0]
    reduced = reduced.astype(jnp.float32)
    attn_sum = reduced[:rows].reshape(blocks, length, shard_width)
    grad_normed = reduced[rows : 2 * rows].reshape(blocks, length, shard_width)
    row_mean = (reduced[2 * rows, :rows] / full_width).reshape(blocks, length, 1)
    gain_term = reduced[2 * rows + 1 : 2 * rows + extra_rows].reshape(full_width)
    mixed_block = ((tokens.astype(jnp.float32) + attn_sum) * live_mask.astype(jnp.float32)).astype(
        jnp.bfloat16
    )
    shard_start = lax.axis_index("tensor") * shard_width
    own_unit = lax.dynamic_slice_in_dim(unit_rows, shard_start, shard_width, 2)
    own_gain = lax.dynamic_slice_in_dim(gain_float, shard_start, shard_width, 0)
    own_grad = inverse_rms * (grad_normed * own_gain - own_unit * row_mean)
    grad_block = (block_grad.astype(jnp.float32) + own_grad).astype(jnp.bfloat16)
    gpack = jnp.concatenate(
        [
            jnp.pad(gain_term.reshape(dp_size, 1, d_local), ((0, 0), (0, 7), (0, 0))),
            grad_query_proj.reshape(dp_size, d_local * q_cols // lane, lane),
            grad_key_proj.reshape(dp_size, d_local * k_cols // lane, lane),
            grad_value_proj.reshape(dp_size, d_local * k_cols // lane, lane),
            grad_output_proj,
        ],
        axis=1,
    ).astype(jnp.bfloat16)
    greduced = lax.psum_scatter(gpack, "dp", scatter_dimension=0, tiled=True)[0].astype(jnp.float32)
    grad_gain = greduced[0]
    grad_wq = greduced[r0:r1].reshape(d_local, q_cols)
    grad_wk = greduced[r1:r2].reshape(d_local, k_cols)
    grad_wv = greduced[r2:r3].reshape(d_local, k_cols)
    grad_wo = greduced[r3:r4]
    return (mixed_block, grad_block, grad_gain, grad_wq, grad_wk, grad_wv, grad_wo)


def solution(mesh):
    return jax.shard_map(
        on_device,
        mesh=mesh,
        in_specs=(
            P("dp", None, "tensor"),
            P("dp", None, "tensor"),
            P(),
            P("dp"),
            P("dp", "tensor"),
            P("dp", "tensor"),
            P("dp", "tensor"),
            P("tensor", "dp"),
        ),
        out_specs=(
            P("dp", None, "tensor"),
            P("dp", None, "tensor"),
            P("dp"),
            P("dp", "tensor"),
            P("dp", "tensor"),
            P("dp", "tensor"),
            P("tensor", "dp"),
        ),
        check_vma=False,
    )
```

profile of v0, /device:TPU:1, one launch (start us, length us, event | category | flops | bytes accessed | tf_op | source)
XLA Modules:
  0.0 626.7 jit_solution(15260371974625475414)
XLA Ops:
  7.3 1.3 dynamic_slice.9
  9.8 1.1 multiply_bitcast_fusion
  10.9 2.0 pad_maximum_fusion.1
  14.0 134.4 %all-gather.4.cloned.1.call-done = bf16[2,2,192,4096]{3,2,1,0:T(8,128)(2,1)} async-done(((bf16[2,2,192,512]{3,2,1,0:T(8,128)(2,1)}), bf16[2,2,192,4096]{3,2,1,0:T(8,128)(2,1)}) %all-gather.4.cloned.1.call-update) | async-done | bytes 6291472 | tf_op jit(solution)/shard_map/all_gather | solution.py:86
  148.4 1.9 slice-done.4
  150.3 2.5 copy.68
  152.8 1.4 copy-done.1
  154.9 87.3 %all-gather.6.cloned.1.call-done = bf16[41216,128]{1,0:T(8,128)(2,1)} async-done(((bf16[1288,128]{1,0:T(8,128)(2,1)}), bf16[41216,128]{1,0:T(8,128)(2,1)}) %all-gather.6.cloned.1.call-update) | async-done | bytes 10551312 | tf_op jit(solution)/shard_map/all_gather | solution.py:73
  242.3 0.8 slice_convert_fusion
  243.1 1.7 fusion.83
  244.8 6.6 %slice_bitcast_fusion = (bf16[32,128,512]{1,2,0:T(8,128)(2,1)}, bf16[32,512,128]{2,1,0:T(8,128)(2,1)}) fusion(bf16[32,1288,128]{2,1,0:T(8,128)(2,1)} %bitcast.235), kind=kLoop, calls=%fused_computation.21 | loop fusion | bytes 16777216 | tf_op jit(solution)/shard_map/btk,jkl->btjl/dot_general | solution.py:110
  251.4 4.2 fusion.44
  255.6 7.5 %reshape.219 = bf16[4096,512,1]{1,0,2:T(8,128)(2,1)} reshape(bf16[32,512,128]{2,1,0:T(8,128)(2,1)} %get-tuple-element.24) | data formatting | bytes 8388608 | tf_op jit(solution)/shard_map/reshape | solution.py:80
  263.1 3.1 fusion.52
  266.3 4.0 fusion.43
  271.0 1.1 fusion.50
  272.1 1.0 fusion.51
  275.5 7.0 %copy.34 = bf16[32,128,512]{2,1,0:T(8,128)(2,1)} copy(bf16[32,128,512]{1,2,0:T(8,128)(2,1)} %get-tuple-element.23) | data formatting | bytes 8388608 | tf_op jit(solution)/shard_map/btk,jkl->btjl/dot_general | solution.py:110
  282.9 4.0 convolution_convert_fusion
  287.0 3.2 copy.67
  290.6 4.1 fusion.86
  294.8 1.0 fusion.70
  296.0 1.0 add_convert_fusion
  297.3 0.9 slice-done.3
  298.2 6.0 fusion.5
  304.2 1.3 reshape.207
  306.8 1.3 reshape.209
  308.1 1.4 copy.69
  310.0 2.3 copy_bitcast_fusion
  312.3 6.2 pad_maximum_fusion
  318.6 0.9 reshape.232
  319.5 6.5 %bitcast_convert_fusion.1 = bf16[4096,512]{1,0:T(8,128)(2,1)} fusion(bf16[2,192,512]{2,1,0:T(8,128)(2,1)S(1)} %copy-done.14, f32[4096]{0:T(1024)S(1)} %bitcast.250, f32[2,192]{1,0:T(2,128)S(1)} %copy-done.27, bf16[2,2,192,4096]{3,2,1,0:T(8,128)(2,1)} %all-gather.4.cloned.1.call-done), kind=kOutput, calls=%fused_computation.1 | convolution fusion | flops 1619001344 | bytes 7751168 | tf_op jit(solution)/shard_map/btd,btk->dk/dot_general | solution.py:138
  326.0 7.9 %reshape.212 = bf16[32,512,128]{2,1,0:T(8,128)(2,1)} reshape(bf16[4096,512]{1,0:T(8,128)(2,1)} %bitcast_convert_fusion.1) | data formatting | bytes 8388608 | tf_op jit(solution)/shard_map/reshape | solution.py:189
  333.9 6.6 %copy.47 = bf16[32,512,128]{1,2,0:T(8,128)(2,1)} copy(bf16[32,512,128]{2,1,0:T(8,128)(2,1)} %reshape.212) | data formatting | bytes 8388608 | tf_op jit(solution)/shard_map/reshape | solution.py:189
  340.5 2.0 bitcast_convert_fusion.3
  342.5 2.3 copy.48
  344.8 4.1 bitcast_convert_fusion.2
  348.9 2.3 copy.49
  351.2 4.7 fusion.7
  355.8 95.5 %reduce-scatter.3.cloned.1.call-done = bf16[1,784,512]{2,1,0:T(8,128)(2,1)} async-done(((bf16[8,784,512]{2,1,0:T(8,128)(2,1)}), bf16[1,784,512]{2,1,0:T(8,128)(2,1)}) %reduce-scatter.3.cloned.1.call-update) | async-done | bytes 802832 | tf_op jit(solution)/shard_map/reduce_scatter | solution.py:172
  452.0 3.2 reshape_reshape.5
  455.2 1.5 pad.22
  456.7 19.6 %concatenate.17 = bf16[32,1288,128]{1,2,0:T(8,128)(2,1)} concatenate(bf16[32,8,128]{1,2,0:T(8,128)(2,1)S(1)} %pad.22, bf16[32,512,128]{1,2,0:T(8,128)(2,1)} %copy.47, bf16[32,128,128]{1,2,0:T(8,128)(2,1)S(1)} %copy-done.6, bf16[32,128,128]{1,2,0:T(8,128)(2,1)S(1)} %copy-done.7, bf16[32,512,128]{1,2,0:T(8,128)(2,1)} %fusion.7), dimensions={1} | concatenate | bytes 21102592 | tf_op jit(solution)/shard_map/concatenate | solution.py:186
  478.0 0.9 multiply_convert_fusion.1
  479.0 2.1 add_convert_fusion.1
  481.1 132.7 %reduce-scatter.5.cloned.1.call-done = bf16[1,1288,128]{1,2,0:T(8,128)(2,1)} async-done(((bf16[32,1288,128]{1,2,0:T(8,128)(2,1)}), bf16[1,1288,128]{1,2,0:T(8,128)(2,1)}) %reduce-scatter.5.cloned.1.call-update) | async-done | bytes 329744 | tf_op jit(solution)/shard_map/reduce_scatter | solution.py:196
  613.8 1.0 convert_element_type.183
  615.7 1.0 slice.94
  (123 shorter events, 15.8 us)
Async XLA Ops:
  7.2 5.8 copy-start.19
  7.2 5.9 copy-start.32
  7.2 5.9 copy-start.22
  7.2 5.9 copy-start.23
  7.2 5.9 copy-start.20
  7.2 141.2 %all-gather.4.cloned.1.call-start = ((), (), s32[]{:S(2)}) async-start(), calls=%async_computation.2 | async-start | bytes 7077888 | tf_op jit(solution)/shard_map/all_gather | solution.py:86
  9.2 0.6 copy-start.30
  12.9 229.4 %all-gather.6.cloned.1.call-start = ((), (), s32[]{:S(2)}) async-start(), calls=%async_computation.5 | async-start | bytes 10881024 | tf_op jit(solution)/shard_map/all_gather | solution.py:73
  13.2 0.7 copy-start.18
  13.9 437.4 %reduce-scatter.3.cloned.1.call-start = ((), (), s32[]{:S(2)}) async-start(), calls=%async_computation.3 | async-start | bytes 7225344 | tf_op jit(solution)/shard_map/reduce_scatter | solution.py:172
  148.4 1.9 slice-start.4
  150.3 3.9 copy-start.1
  154.9 117.2 %copy-start.25 = (f32[2,192]{1,0:T(2,128)}, f32[2,192]{1,0:T(2,128)S(1)}, u32[]{:S(2)}) copy-start(f32[2,192]{1,0:T(2,128)S(1)} %add_rsqrt_fusion) | copy-start | bytes 4612
  244.8 27.3 %copy-start.8 = (bf16[32,128,128]{2,1,0:T(8,128)(2,1)}, bf16[32,128,128]{2,1,0:T(8,128)(2,1)S(1)}, u32[]{:S(2)}) copy-start(bf16[32,128,128]{2,1,0:T(8,128)(2,1)S(1)} %get-tuple-element.25) | copy-start | bytes 3145732
  244.8 6.6 %copy-start.2 = (bf16[48,8,32,128]{3,2,1,0:T(8,128)(2,1)S(1)}, bf16[48,8,32,128]{3,2,1,0:T(8,128)(2,1)}, u32[]{:S(2)}) copy-start(bf16[48,8,32,128]{3,2,1,0:T(8,128)(2,1)} %copy.68) | copy-start | bytes 9437188
  263.1 3.1 copy-start
  263.1 8.9 %slice-start = ((s8[6291456]{0:T(1024)(128)(4,1)}), s8[4194304]{0:T(1024)(128)(4,1)S(1)}, s32[]{:S(2)}) async-start(s8[6291456]{0:T(1024)(128)(4,1)} %bitcast.224), calls=%async_computation.6 | async-start | bytes 8388608
  266.3 5.8 slice-start.1
  275.0 19.8 %copy-start.16 = (bf16[2,128,192]{1,2,0:T(8,128)(2,1)}, bf16[2,128,192]{1,2,0:T(8,128)(2,1)S(1)}, u32[]{:S(2)}) copy-start(bf16[2,128,192]{1,2,0:T(8,128)(2,1)S(1)} %fusion.49) | copy-start | bytes 294916
  290.6 4.2 copy-start.13
  294.8 1.2 copy-start.9
  294.8 1.2 copy-start.21
  294.8 2.5 slice-start.2
  296.0 2.2 slice-start.3
  296.0 2.2 copy-start.26
  308.1 1.4 copy-start.24
  308.1 1.4 copy-start.29
  308.1 1.9 copy-start.4
  318.5 1.0 copy-start.14
  318.5 1.0 copy-start.27
  318.5 295.3 %reduce-scatter.5.cloned.1.call-start = ((), (), s32[]{:S(2)}) async-start(), calls=%async_computation.4 | async-start | bytes 11894784 | tf_op jit(solution)/shard_map/reduce_scatter | solution.py:196
  333.9 6.6 %copy-start.10 = (bf16[2,24,32,8,128]{4,3,2,1,0:T(8,128)(2,1)S(1)}, bf16[2,24,32,8,128]{4,3,2,1,0:T(8,128)(2,1)}, u32[]{:S(2)}) copy-start(bf16[2,24,32,8,128]{4,3,2,1,0:T(8,128)(2,1)} %get-tuple-element.27) | copy-start | bytes 9437188
  333.9 6.6 %copy-start.17 = (bf16[2,128,192]{1,2,0:T(8,128)(2,1)S(1)}, bf16[2,128,192]{1,2,0:T(8,128)(2,1)}, u32[]{:S(2)}) copy-start(bf16[2,128,192]{1,2,0:T(8,128)(2,1)} %copy-done.16) | copy-start | bytes 294916
  344.8 6.3 %copy-start.3 = (bf16[48,8,32,128]{3,2,1,0:T(8,128)(2,1)S(1)}, bf16[48,8,32,128]{3,2,1,0:T(8,128)(2,1)}, u32[]{:S(2)}) copy-start(bf16[48,8,32,128]{3,2,1,0:T(8,128)(2,1)} %copy.68) | copy-start | bytes 9437188
  344.8 6.3 %copy-start.15 = (bf16[2,192,512,1]{2,1,0,3:T(8,128)(2,1)S(1)}, bf16[2,192,512,1]{2,1,0,3:T(8,128)(2,1)}, u32[]{:S(2)}) copy-start(bf16[2,192,512,1]{2,1,0,3:T(8,128)(2,1)} %reshape.232) | copy-start | bytes 1179652
  355.8 100.9 %copy-start.6 = (bf16[32,128,128]{1,2,0:T(8,128)(2,1)S(1)}, bf16[32,128,128]{1,2,0:T(8,128)(2,1)}, u32[]{:S(2)}) copy-start(bf16[32,128,128]{1,2,0:T(8,128)(2,1)} %copy.48) | copy-start | bytes 3145732
  355.8 100.9 %copy-start.7 = (bf16[32,128,128]{1,2,0:T(8,128)(2,1)S(1)}, bf16[32,128,128]{1,2,0:T(8,128)(2,1)}, u32[]{:S(2)}) copy-start(bf16[32,128,128]{1,2,0:T(8,128)(2,1)} %copy.49) | copy-start | bytes 3145732
  476.3 1.2 copy-start.5
  476.4 1.7 copy-start.12
  477.5 1.5 copy-start.11
  477.5 1.5 copy-start.28
  477.5 1.5 copy-start.31
Sparse Core Ops, SparseCore 0:
  13.0 135.3 all-gather.3
  151.6 90.6 all-gather.5
  318.7 132.6 reduce-scatter.2
  476.5 137.2 reduce-scatter.4
where the time goes:
time: 637 us; the launch traced here: 627 us
  waiting for transfers between devices  450 us (71%)
  local copies, waits for them, and re-layouts  95.7 us (15%)
  matrix products  43 us (7%)
  other arithmetic  23.3 us (4%)
  between operations  14.5 us (2%)
    all_gather x1, waiting for transfers between devices, on_device(): lax.all_gather(jnp.stack([tokens, block_grad]), 'tensor', axis=3, tiled=T...  134 us
    reduce_scatter x1, waiting for transfers between devices, on_device(): lax.psum_scatter(gpack, 'dp', scatter_dimension=0, tiled=True)[0]  133 us
    reduce_scatter x1, waiting for transfers between devices, on_device(): lax.psum_scatter(payload, 'tensor', scatter_dimension=0, tiled=True)[0]  95.5 us
    all_gather x1, waiting for transfers between devices, on_device(): packed = lax.all_gather(pack, 'dp', axis=0, tiled=False)  87.3 us
    concatenate x1, local copies, waits for them, and re-layouts, on_device(): jnp.concatenate([jnp.pad(gain_term.reshape(dp_size, 1, d_local), ((0, 0),...  19.6 us
    reshape x2, local copies, waits for them, and re-layouts, on_device(): grad_query_proj.reshape(dp_size, d_local * q_cols // lane, lane)  14.5 us
    unnamed x84, local copies, waits for them, and re-layouts  14.5 us
    dot_general x2, local copies, waits for them, and re-layouts, on_device(): jnp.einsum('btk,jkl->btjl', context_flat, wo_blk, preferred_element_type=...  13.5 us
  transfers between devices with their start and end apart: 4, of which 4 were waited for; matrix products, arithmetic and copies ran while one was open for 7% of the time, Pallas kernels for 0%

commit v1 on v0

--- a/solution.py
+++ b/solution.py
@@ -83,7 +83,10 @@
     wo_blk = packed[:, r3:r4, :]
     live_mask = (jnp.arange(blocks) < own_count).astype(jnp.bfloat16)[:, None, None]
     block_grad = grad_out * live_mask
-    both = lax.all_gather(jnp.stack([tokens, block_grad]), "tensor", axis=3, tiled=True)
+    _open_positions = lambda row_data, a_name: jnp.concatenate(
+        lax.all_to_all(jnp.stack([row_data] * lax.axis_size(a_name)), a_name, 0, 0), axis=3
+    )
+    both = _open_positions(jnp.stack([tokens, block_grad]), "tensor")
     wide_in, upstream = (both[0], both[1])
     repeat = HEADS // KV
     kv_local = wk_all.shape[1] // HD

time: 637 us -> 597 us (0.937)
  waiting for transfers between devices: 450 us -> 356 us
  local copies, waits for them, and re-layouts: 95.7 us -> 131 us
  other arithmetic: 23.3 us -> 33.3 us
    all_gather x1 -> x0, waiting for transfers between devices: 134 us -> none  [on_device(): lax.all_gather(jnp.stack([tokens, block_grad]), 'tensor', axis=3, tiled=T...]
    all_to_all x0 -> x1, waiting for transfers between devices: none -> 124 us  [on_device(): lax.all_to_all(jnp.stack([row_data] * lax.axis_size(a_name)), a_name, 0, 0)]
    all_gather x1, waiting for transfers between devices: 87.3 us -> 0.02 us  [on_device(): packed = lax.all_gather(pack, 'dp', axis=0, tiled=False)]
    convert_element_type x0 -> x5, local copies, waits for them, and re-layouts: none -> 21.5 us  [the longest x2 13.9 us: on_device(): wide_float = wide_in.astype(jnp.float32)]
    convert_element_type x0 -> x2, other arithmetic: none -> 8.34 us  [the longest x1 5.56 us: on_device(): wide_float = wide_in.astype(jnp.float32)]
    another operation x2 -> x4, local copies, waits for them, and re-layouts: 4.55 us -> 11.8 us
    unnamed x84 -> x61, local copies, waits for them, and re-layouts: 14.5 us -> 13.3 us
  transfers between devices with their start and end apart: 4 -> 4, of which waited for: 4 -> 3; matrix products, arithmetic and copies ran while one was open for 7% -> 13% of each run, Pallas kernels for 0% -> 0%
where the time goes in v1:
time: 597 us; the launch traced here: 590 us
  waiting for transfers between devices  356 us (60%)
  local copies, waits for them, and re-layouts  131 us (22%)
  matrix products  48.4 us (8%)
  other arithmetic  33.3 us (6%)
  between operations  14.5 us (2%)
  starting transfers between devices  6.48 us (1%)
    reduce_scatter x1, waiting for transfers between devices, on_device(): lax.psum_scatter(gpack, 'dp', scatter_dimension=0, tiled=True)[0]  133 us
    all_to_all x1, waiting for transfers between devices, on_device(): lax.all_to_all(jnp.stack([row_data] * lax.axis_size(a_name)), a_name, 0, 0)  124 us
    reduce_scatter x1, waiting for transfers between devices, on_device(): lax.psum_scatter(payload, 'tensor', scatter_dimension=0, tiled=True)[0]  99.5 us
    concatenate x1, local copies, waits for them, and re-layouts, on_device(): jnp.concatenate([jnp.pad(gain_term.reshape(dp_size, 1, d_local), ((0, 0),...  19.6 us
    reshape x2, local copies, waits for them, and re-layouts, on_device(): grad_query_proj.reshape(dp_size, d_local * q_cols // lane, lane)  14.3 us
    convert_element_type x2, local copies, waits for them, and re-layouts, on_device(): wide_float = wide_in.astype(jnp.float32)  13.9 us
    unnamed x61, local copies, waits for them, and re-layouts  13.3 us
    dot_general x2, local copies, waits for them, and re-layouts, on_device(): jnp.einsum('btk,jkl->btjl', context_flat, wo_blk, preferred_element_type=...  12.4 us
  transfers between devices with their start and end apart: 4, of which 3 were waited for; matrix products, arithmetic and copies ran while one was open for 13% of the time, Pallas kernels for 0%

profile of v1, /device:TPU:1, one launch (start us, length us, event | category | flops | bytes accessed | tf_op | source)
XLA Modules:
  0.0 589.6 jit_solution(17397916263425329936)
XLA Ops:
  12.1 1.2 dynamic_slice.9
  16.2 3.3 stack.11
  19.5 6.4 %all-to-all-start = ((bf16[8,2,2,192,512]{4,3,2,1,0:T(8,128)(2,1)}), bf16[8,2,2,192,512]{4,3,2,1,0:T(8,128)(2,1)}, u32[]{:S(2)}, u32[]{:S(2)}) async-start(bf16[8,2,2,192,512]{4,3,2,1,0:T(8,128)(2,1)} %stack.11), calls=%async_computation | async-start | bytes 12582912 | tf_op jit(solution)/shard_map/all_to_all | solution.py:87
  26.0 123.5 %all-to-all-done = bf16[8,2,2,192,512]{4,3,2,1,0:T(8,128)(2,1)} async-done(((bf16[8,2,2,192,512]{4,3,2,1,0:T(8,128)(2,1)}), bf16[8,2,2,192,512]{4,3,2,1,0:T(8,128)(2,1)}, u32[]{:S(2)}, u32[]{:S(2)}) %all-to-all-start) | async-done | bytes 6291488 | tf_op jit(solution)/shard_map/all_to_all | solution.py:87
  149.5 5.6 slice_convert_fusion
  155.0 6.3 %copy.93 = f32[1,2,192,8,512]{4,3,2,1,0:T(8,128)} copy(f32[1,2,192,8,512]{4,2,1,0,3:T(8,128)S(1)} %get-tuple-element.43) | data formatting | bytes 12582912 | tf_op jit(solution)/shard_map/convert_element_type | solution.py:93
  161.3 7.7 %reshape.237 = f32[2,192,4096]{2,1,0:T(8,128)} reshape(f32[1,2,192,8,512]{4,3,2,1,0:T(8,128)} %copy.93) | data formatting | bytes 12582912 | tf_op jit(solution)/shard_map/convert_element_type | solution.py:93
  169.0 3.6 copy.85
  172.6 3.8 reshape_squeeze.4
  176.4 2.6 multiply_reduce_fusion
  180.8 3.1 fusion.74
  183.9 5.9 %slice_bitcast_fusion = (bf16[32,128,512]{1,2,0:T(8,128)(2,1)}, bf16[32,512,128]{2,1,0:T(8,128)(2,1)}) fusion(bf16[32,1288,128]{2,1,0:T(8,128)(2,1)} %bitcast.215), kind=kLoop, calls=%fused_computation.16 | loop fusion | bytes 16777216 | tf_op jit(solution)/shard_map/btk,jkl->btjl/dot_general | solution.py:113
  189.8 2.8 multiply_convert_fusion
  192.6 3.4 copy.79
  196.0 4.2 convert_element_type.159
  200.2 2.3 fusion.46
  204.4 5.0 fusion.38
  209.3 7.7 %reshape.242 = bf16[4096,512,1]{1,0,2:T(8,128)(2,1)} reshape(bf16[32,512,128]{2,1,0:T(8,128)(2,1)} %get-tuple-element.40) | data formatting | bytes 8388608 | tf_op jit(solution)/shard_map/reshape | solution.py:80
  217.0 4.0 fusion.37
  223.1 1.3 fusion.35
  226.3 1.2 fusion.36
  227.5 6.5 %copy.83 = bf16[32,128,512]{2,1,0:T(8,128)(2,1)} copy(bf16[32,128,512]{1,2,0:T(8,128)(2,1)} %get-tuple-element.39) | data formatting | bytes 8388608 | tf_op jit(solution)/shard_map/btk,jkl->btjl/dot_general | solution.py:113
  234.0 1.3 copy.82
  236.2 4.1 convolution_convert_fusion
  240.4 3.0 copy.118
  244.5 1.9 reshape.225
  246.4 4.2 fusion.77
  251.6 5.8 fusion.6
  257.5 4.5 fusion
  262.0 1.3 reshape.229
  264.6 1.3 reshape.231
  265.9 3.5 copy.119
  269.4 2.3 copy_bitcast_fusion
  271.7 6.2 %pad_maximum_fusion = bf16[8,784,512]{2,1,0:T(8,128)(2,1)} fusion(bf16[8,16,512]{2,1,0:T(8,128)(2,1)S(1)} %broadcast_in_dim.12, bf16[8,384,512]{2,1,0:T(8,128)(2,1)S(1)} %get-tuple-element.54, bf16[8,384,512]{2,1,0:T(8,128)(2,1)S(1)} %get-tuple-element.55), kind=kLoop, calls=%fused_computation.4 | loop fusion | flops 19267584 | bytes 12845056 | tf_op jit(solution)/shard_map/concatenate | solution.py:167
  278.9 3.9 bitcast_convert_fusion.2
  282.8 2.5 copy.100
  285.3 4.0 bitcast_convert_fusion.3
  289.3 2.3 copy.99
  291.5 4.4 bitcast_convert_fusion.1
  295.9 7.6 %reshape.234 = bf16[32,512,128]{2,1,0:T(8,128)(2,1)} reshape(bf16[4096,512]{1,0:T(8,128)(2,1)} %bitcast_convert_fusion.1) | data formatting | bytes 8388608 | tf_op jit(solution)/shard_map/reshape | solution.py:192
  303.6 6.6 %copy.98 = bf16[32,512,128]{1,2,0:T(8,128)(2,1)} copy(bf16[32,512,128]{2,1,0:T(8,128)(2,1)} %reshape.234) | data formatting | bytes 8388608 | tf_op jit(solution)/shard_map/reshape | solution.py:192
  310.2 4.7 fusion.2
  314.9 99.5 %reduce-scatter.3.cloned.1.call-done = bf16[1,784,512]{2,1,0:T(8,128)(2,1)} async-done(((bf16[8,784,512]{2,1,0:T(8,128)(2,1)}), bf16[1,784,512]{2,1,0:T(8,128)(2,1)}) %reduce-scatter.3.cloned.1.call-update) | async-done | bytes 802832 | tf_op jit(solution)/shard_map/reduce_scatter | solution.py:175
  415.1 3.2 reshape_reshape.5
  418.3 1.5 pad.22
  419.8 19.6 %concatenate.17 = bf16[32,1288,128]{1,2,0:T(8,128)(2,1)} concatenate(bf16[32,8,128]{1,2,0:T(8,128)(2,1)S(1)} %pad.22, bf16[32,512,128]{1,2,0:T(8,128)(2,1)} %copy.98, bf16[32,128,128]{1,2,0:T(8,128)(2,1)S(1)} %copy-done.9, bf16[32,128,128]{1,2,0:T(8,128)(2,1)S(1)} %copy-done.8, bf16[32,512,128]{1,2,0:T(8,128)(2,1)} %fusion.2), dimensions={1} | concatenate | bytes 21102592 | tf_op jit(solution)/shard_map/concatenate | solution.py:189
  442.0 2.1 add_convert_fusion.1
  444.2 132.6 %reduce-scatter.5.cloned.1.call-done = bf16[1,1288,128]{1,2,0:T(8,128)(2,1)} async-done(((bf16[32,1288,128]{1,2,0:T(8,128)(2,1)}), bf16[1,1288,128]{1,2,0:T(8,128)(2,1)}) %reduce-scatter.5.cloned.1.call-update) | async-done | bytes 329744 | tf_op jit(solution)/shard_map/reduce_scatter | solution.py:199
  (106 shorter events, 30.0 us)
Async XLA Ops:
  7.2 171.8 %all-gather.3.cloned.1.call-start = ((), (), s32[]{:S(2)}) async-start(), calls=%async_computation.5 | async-start | bytes 10881024 | tf_op jit(solution)/shard_map/all_gather | solution.py:73
  11.4 0.7 copy-start.16
  14.0 1.1 copy-start.23
  19.5 130.0 %all-to-all-start = ((bf16[8,2,2,192,512]{4,3,2,1,0:T(8,128)(2,1)}), bf16[8,2,2,192,512]{4,3,2,1,0:T(8,128)(2,1)}, u32[]{:S(2)}, u32[]{:S(2)}) async-start(bf16[8,2,2,192,512]{4,3,2,1,0:T(8,128)(2,1)} %stack.11), calls=%async_computation | async-start | bytes 12582912 | tf_op jit(solution)/shard_map/all_to_all | solution.py:87
  25.9 388.5 %reduce-scatter.3.cloned.1.call-start = ((), (), s32[]{:S(2)}) async-start(), calls=%async_computation.3 | async-start | bytes 7225344 | tf_op jit(solution)/shard_map/reduce_scatter | solution.py:175
  179.0 10.8 %copy-start.18 = (f32[2,192]{1,0:T(2,128)}, f32[2,192]{1,0:T(2,128)S(1)}, u32[]{:S(2)}) copy-start(f32[2,192]{1,0:T(2,128)S(1)} %add_rsqrt_fusion) | copy-start | bytes 4612
  200.2 2.3 copy-start.4
  202.5 1.9 copy-start.1
  221.0 1.0 copy-start.25
  240.3 3.1 copy-start.11
  246.4 4.2 copy-start.6
  246.4 4.2 copy-start.15
  250.6 1.0 copy-start.19
  251.6 5.9 copy-start.5
  251.6 5.9 copy-start.17
  257.5 4.5 copy-start
  265.9 3.5 copy-start.21
  265.9 3.5 copy-start.22
  265.9 3.5 copy-start.3
  278.0 298.8 %reduce-scatter.5.cloned.1.call-start = ((), (), s32[]{:S(2)}) async-start(), calls=%async_computation.4 | async-start | bytes 11894784 | tf_op jit(solution)/shard_map/reduce_scatter | solution.py:199
  285.3 6.2 %copy-start.13 = (bf16[2,192,512]{2,1,0:T(8,128)(2,1)S(1)}, bf16[2,192,512]{2,1,0:T(8,128)(2,1)}, u32[]{:S(2)}) copy-start(bf16[2,192,512]{2,1,0:T(8,128)(2,1)} %reshape.225) | copy-start | bytes 1179652
  303.6 6.7 %copy-start.2 = (bf16[2,192,32,128]{3,2,1,0:T(8,128)(2,1)S(1)}, bf16[2,192,32,128]{3,2,1,0:T(8,128)(2,1)}, u32[]{:S(2)}) copy-start(bf16[2,192,32,128]{3,2,1,0:T(8,128)(2,1)} %reshape_squeeze.4) | copy-start | bytes 9437188
  303.6 6.7 %copy-start.14 = (bf16[2,192,512,1]{2,1,0,3:T(8,128)(2,1)S(1)}, bf16[2,192,512,1]{2,1,0,3:T(8,128)(2,1)}, u32[]{:S(2)}) copy-start(bf16[2,192,512,1]{2,1,0,3:T(8,128)(2,1)} %reshape.255) | copy-start | bytes 1179652
  314.9 104.9 %copy-start.8 = (bf16[32,128,128]{1,2,0:T(8,128)(2,1)S(1)}, bf16[32,128,128]{1,2,0:T(8,128)(2,1)}, u32[]{:S(2)}) copy-start(bf16[32,128,128]{1,2,0:T(8,128)(2,1)} %copy.100) | copy-start | bytes 3145732
  314.9 104.9 %copy-start.9 = (bf16[32,128,128]{1,2,0:T(8,128)(2,1)S(1)}, bf16[32,128,128]{1,2,0:T(8,128)(2,1)}, u32[]{:S(2)}) copy-start(bf16[32,128,128]{1,2,0:T(8,128)(2,1)} %copy.99) | copy-start | bytes 3145732
  439.4 1.2 copy-start.7
  439.4 1.7 copy-start.12
  440.5 1.5 copy-start.10
  440.6 1.5 copy-start.20
  440.6 1.5 copy-start.24
Sparse Core Ops, SparseCore 0:
  12.2 117.6 all-gather.2
  278.1 136.2 reduce-scatter.2
  439.5 137.1 reduce-scatter.4
